TPU v7x, 128 devices: a whole 4x4x4 slice. The times are simulated.
128 devices in a mesh: req: 16 (over z, y), mp: 8 (over x, core).
Axes of the slice: x: 4, y: 4, z: 4, core: 2. Of those that a mesh axis runs over, the one named last changes fastest.
Arguments:
- q_pre: bfloat16 [8192, 3072], P('req', 'mp'), may hold values from -64 to 64
- k_pre: bfloat16 [8192, 1024], P('req', 'mp'), may hold values from -64 to 64
- v_pre: bfloat16 [8192, 1024], P('req', 'mp'), may hold values from -12 to 12
- q_bias: float32 [3072], P('mp'), may hold values from -3 to 3
- k_bias: float32 [1024], P('mp'), may hold values from -3 to 3
- v_bias: float32 [1024], P('mp'), may hold values from -3 to 3
- segment_ids: int32 [8192], P('req'), may hold values from -1 to 63, as said below
- lengths: int32 [16, 4], replicated, may hold values from 64 to 128, as said below
- page_table: int32 [16, 4], replicated, may hold values from 0 to 63, as said below
- w_out: bfloat16 [3072, 5120], P('mp'), may hold values from -0.109375 to 0.109375
- residual: bfloat16 [8192, 5120], P('req'), may hold values from -4 to 4
- norm_gain: float32 [5120], replicated, may hold values from 0.1 to 1.9
- w_gate: bfloat16 [5120, 6912], P('req', 'mp'), may hold values from -0.078125 to 0.078125
- w_up: bfloat16 [5120, 6912], P('req', 'mp'), may hold values from -0.078125 to 0.078125
Outputs:
- hidden: bfloat16 [8192, 6912], P('req', 'mp')
- kv_cache: bfloat16 [64, 8, 128, 256], P('req', 'mp')
Inputs may be any that keep to these rules, and one draw needn't show every extreme that they name: Requests of block r lie in order from the block's first token, request j taking lengths[r, j] tokens; in every block one request has exactly 128 tokens. `segment_ids`: token t of block r carries r * 4 + j inside request j's run of tokens given by lengths, and -1 after the last request of its block. `page_table`: every page is named once; page p is held by req index p // 4; the requests of one block have pages held by different req indices.
All inputs are finite; a program needn't handle non-finite values.
Results may differ from a plain program's by a relative error of at most 0.019.
Values may be sent and summed in bfloat16 or wider, within the bound.
A program may use at most 128 MiB of HBM per device.

v0:
```python
import math
import jax
import jax.numpy as jnp
from jax import lax
from jax.sharding import PartitionSpec as P

HD = 128
PAGE = 128
REQS = 4
THETA = 1000000.0
EPS = 1e-06


def rotate(values, positions):
    half_dim = values.shape[-1] // 2
    frequencies = THETA ** (-jnp.arange(half_dim, dtype=jnp.float32) * (2.0 / values.shape[-1]))
    angles = positions[:, None] * frequencies[None, :]
    cosine = jnp.cos(angles)[:, None, :]
    sine_part = jnp.sin(angles)[:, None, :]
    first_half = values[..., :half_dim]
    second = values[..., half_dim:]
    return jnp.concatenate(
        [first_half * cosine - second * sine_part, second * cosine + first_half * sine_part],
        axis=-1,
    )


def normalize(resid_rows, summed, gain_row):
    state = resid_rows.astype(jnp.float32) + summed
    scale_row = lax.rsqrt(jnp.mean(state * state, axis=-1, keepdims=True) + EPS)
    return (state * scale_row * gain_row).astype(jnp.bfloat16)


def shards(
    q_pre,
    k_pre,
    v_pre,
    q_bias,
    k_bias,
    v_bias,
    segment_ids,
    lengths,
    page_table,
    w_out,
    residual,
    norm_gain,
    w_gate,
    w_up,
):
    me_req = lax.axis_index("req")
    groups_all = lax.axis_size("req")
    block_rows = q_pre.shape[0]
    kv_heads = k_pre.shape[1] // HD
    q_heads = q_pre.shape[1] // HD
    group_size = q_heads // kv_heads
    wg_full = lax.all_gather(w_gate, "req", axis=0, tiled=True)
    wu_full = lax.all_gather(w_up, "req", axis=0, tiled=True)
    own_lens = lax.dynamic_index_in_dim(lengths, me_req, 0, keepdims=False)
    own_pages = lax.dynamic_index_in_dim(page_table, me_req, 0, keepdims=False)
    own_owner = own_pages // REQS
    starts = jnp.cumsum(own_lens) - own_lens
    alive = segment_ids >= 0
    req_idx = jnp.clip(segment_ids - me_req * REQS, 0, REQS - 1)
    req_hit = req_idx[:, None] == jnp.arange(REQS)[None, :]
    row_start = jnp.sum(jnp.where(req_hit, starts[None, :], 0), axis=1)
    token = jnp.arange(block_rows, dtype=jnp.int32)
    positions = (token - row_start).astype(jnp.float32)
    keep = alive[:, None, None]
    queries = rotate(
        (q_pre.astype(jnp.float32) + q_bias).reshape(block_rows, q_heads, HD), positions
    )
    queries = jnp.where(keep, queries, 0.0).astype(jnp.bfloat16)
    keys = rotate((k_pre.astype(jnp.float32) + k_bias).reshape(block_rows, kv_heads, HD), positions)
    keys = jnp.where(keep, keys, 0.0).astype(jnp.bfloat16)
    values = (v_pre.astype(jnp.float32) + v_bias).reshape(block_rows, kv_heads, HD)
    values = jnp.where(keep, values, 0.0).astype(jnp.bfloat16)
    scale_factor = 1.0 / math.sqrt(HD)
    q_groups = queries.reshape(block_rows, kv_heads, group_size, HD)
    scores = (
        jnp.einsum("qhge,khe->hgqk", q_groups, keys, preferred_element_type=jnp.float32)
        * scale_factor
    )
    allowed = (
        (segment_ids[:, None] == segment_ids[None, :])
        & alive[None, :]
        & (token[None, :] <= token[:, None])
    )[None, None]
    row_max = jnp.max(jnp.where(allowed, scores, -1e30), axis=-1, keepdims=True)
    weights = jnp.where(allowed, jnp.exp(scores - row_max), 0.0)
    row_sum = jnp.sum(weights, axis=-1, keepdims=True)
    present = alive[None, None, :, None]
    probs = jnp.where(present, weights / jnp.where(present, row_sum, 1.0), 0.0).astype(jnp.bfloat16)
    attended = jnp.einsum("hgqk,khe->qhge", probs, values, preferred_element_type=jnp.float32)
    attended = attended.astype(jnp.bfloat16).reshape(block_rows, q_heads * HD)
    kv_rows = jnp.concatenate([keys, values], axis=-1)
    kv_rows = jnp.pad(kv_rows, ((0, PAGE), (0, 0), (0, 0)))
    slot = jnp.arange(PAGE, dtype=jnp.int32)
    pages = []
    for j in range(REQS):
        page = lax.dynamic_slice_in_dim(kv_rows, starts[j], PAGE, axis=0)
        page = jnp.where((slot < own_lens[j])[:, None, None], page, jnp.zeros((), jnp.bfloat16))
        pages.append(page)
    pages = jnp.stack(pages)
    to_owner = (own_owner[None, :] == jnp.arange(groups_all)[:, None]).astype(jnp.bfloat16)
    kv_send = jnp.einsum(
        "gj,jphc->gphc", to_owner, pages, preferred_element_type=jnp.float32
    ).astype(jnp.bfloat16)
    kv_in = lax.all_to_all(kv_send, "req", split_axis=0, concat_axis=0, tiled=True)
    hits = (
        page_table[None, :, :] == (me_req * REQS + jnp.arange(REQS, dtype=jnp.int32))[:, None, None]
    )
    page_select = jnp.sum(hits.astype(jnp.int32), axis=2).astype(jnp.bfloat16)
    cache_out = jnp.einsum(
        "ls,sphc->lhpc", page_select, kv_in, preferred_element_type=jnp.float32
    ).astype(jnp.bfloat16)
    summed = lax.psum(
        jnp.dot(attended, w_out, preferred_element_type=jnp.float32).astype(jnp.bfloat16), "mp"
    ).astype(jnp.float32)
    normed = normalize(residual, summed, norm_gain)
    gate_acc = jnp.dot(normed, wg_full, preferred_element_type=jnp.float32)
    up_acc = jnp.dot(normed, wu_full, preferred_element_type=jnp.float32)
    hidden = (jax.nn.silu(gate_acc) * up_acc).astype(jnp.bfloat16)
    return (hidden, cache_out)


def solution(mesh):
    in_specs = (
        P("req", "mp"),
        P("req", "mp"),
        P("req", "mp"),
        P("mp"),
        P("mp"),
        P("mp"),
        P("req"),
        P(),
        P(),
        P("mp", None),
        P("req", None),
        P(),
        P("req", "mp"),
        P("req", "mp"),
    )
    out_specs = (P("req", "mp"), P("req", "mp", None, None))
    return jax.shard_map(shards, mesh=mesh, in_specs=in_specs, out_specs=out_specs, check_vma=False)
```

profile of v0, /device:TPU:1, one launch (start us, length us, event | category | flops | bytes accessed | tf_op | source)
XLA Modules:
  0.0 211.2 jit_solution(10629385373972112505)
XLA Ops:
  8.1 0.9 fusion.45
  9.2 0.7 broadcast_compare_fusion
  9.9 0.7 subtract_clamp_fusion
  10.7 1.2 copy.81
  12.4 0.9 add_bitcast_fusion
  13.3 1.2 fusion.28
  14.6 1.0 fusion.15
  15.6 0.8 convert_add_fusion.1
  16.6 0.8 fusion
  17.4 0.7 fusion.3
  18.1 1.2 fusion.9
  19.3 0.9 copy-done
  20.2 4.7 %convolution_convert_fusion = bf16[512,5120]{1,0:T(8,128)(2,1)} fusion(bf16[512,384]{0,1:T(8,128)(2,1)S(1)} %bitcast.97, bf16[384,5120]{1,0:T(8,128)(2,1)S(1)} %copy-done), kind=kOutput, calls=%fused_computation.3 | convolution fusion | flops 2015887360 | bytes 9568256 | tf_op jit(solution)/shard_map/dot_general | solution.py:117
  25.6 0.5 all-gather.5.cloned.1.call-update
  26.2 0.7 fusion.60
  34.6 0.7 fusion.59
  35.3 0.6 iota_compare_fusion.4
  35.9 0.7 iota_compare_fusion.5
  36.6 0.6 iota_compare_fusion.6
  37.3 0.7 iota_compare_fusion.7
  38.9 0.9 fusion.8
  39.8 1.4 copy.89
  41.2 8.6 %all-to-all-start = ((bf16[16,128,1,256]{3,1,2,0:T(8,128)(2,1)}), bf16[16,128,1,256]{3,1,2,0:T(8,128)(2,1)S(1)}, u32[]{:S(2)}, u32[]{:S(2)}) async-start(bf16[16,128,1,256]{3,1,2,0:T(8,128)(2,1)} %copy.89), calls=%async_computation | async-start | bytes 2097152 | tf_op jit(solution)/shard_map/all_to_all | solution.py:108
  49.9 18.8 %all-to-all-done = bf16[16,128,1,256]{3,1,2,0:T(8,128)(2,1)S(1)} async-done(((bf16[16,128,1,256]{3,1,2,0:T(8,128)(2,1)}), bf16[16,128,1,256]{3,1,2,0:T(8,128)(2,1)S(1)}, u32[]{:S(2)}, u32[]{:S(2)}) %all-to-all-start) | async-done | bytes 1048608 | tf_op jit(solution)/shard_map/all_to_all | solution.py:108
  68.7 0.7 fusion.12
  69.4 0.7 copy.91
  70.1 35.0 %all-reduce.3.cloned.1.call-done = bf16[512,5120]{1,0:T(8,128)(2,1)} async-done(((bf16[512,5120]{1,0:T(8,128)(2,1)}), bf16[512,5120]{1,0:T(8,128)(2,1)}) %all-reduce.3.cloned.1.call-update) | async-done | bytes 5242896 | tf_op jit(solution)/shard_map/psum | solution.py:116
  105.2 5.8 %multiply_reduce_fusion = f32[512]{0:T(512)S(1)} fusion(bf16[512,5120]{1,0:T(8,128)(2,1)} %all-reduce.3.cloned.1.call-done, bf16[512,5120]{1,0:T(8,128)(2,1)} %param.24), kind=kLoop, calls=%fused_computation.1 | loop fusion | flops 13106688 | bytes 10487808 | tf_op jit(solution)/shard_map/reduce_sum | solution.py:30
  111.0 3.9 %all-gather.3.cloned.1.call-done = bf16[5120,864]{1,0:T(8,128)(2,1)} async-done(((bf16[320,864]{1,0:T(8,128)(2,1)}), bf16[5120,864]{1,0:T(8,128)(2,1)}) %all-gather.3.cloned.1.call-update) | async-done | bytes 8847376 | tf_op jit(solution)/shard_map/all_gather | solution.py:56
  114.9 12.1 %fusion.58 = f32[512,864]{0,1:T(8,128)S(1)} fusion(bf16[5120,864]{1,0:T(8,128)(2,1)} %all-gather.3.cloned.1.call-done, bf16[512,5120]{1,0:T(8,128)(2,1)} %all-reduce.3.cloned.1.call-done, bf16[512,5120]{1,0:T(8,128)(2,1)} %param.24, f32[5120]{0:T(1024)S(1)} %copy-done.4, f32[512]{0:T(512)S(1)} %add_rsqrt_fusion), kind=kOutput, calls=%fused_computation.105 | convolution fusion | flops 4545576960 | bytes 21125120 | tf_op jit(solution)/shard_map/dot_general | solution.py:120
  127.0 64.0 %all-gather.5.cloned.1.call-done = bf16[5120,864]{1,0:T(8,128)(2,1)} async-done(((bf16[320,864]{1,0:T(8,128)(2,1)}), bf16[5120,864]{1,0:T(8,128)(2,1)}) %all-gather.5.cloned.1.call-update) | async-done | bytes 8847376 | tf_op jit(solution)/shard_map/all_gather | solution.py:57
  191.0 12.7 %multiply_convert_fusion.1 = bf16[512,864]{0,1:T(8,128)(2,1)} fusion(f32[512,864]{0,1:T(8,128)S(1)} %fusion.58, bf16[5120,864]{1,0:T(8,128)(2,1)} %all-gather.5.cloned.1.call-done, bf16[512,5120]{1,0:T(8,128)(2,1)} %all-reduce.3.cloned.1.call-done, bf16[512,5120]{1,0:T(8,128)(2,1)} %param.24, f32[5120]{0:T(1024)S(1)} %copy-done.4, f32[512]{0:T(512)S(1)} %add_rsqrt_fusion), kind=kOutput, calls=%fused_computation.11 | convolution fusion | flops 4548231168 | bytes 22009856 | tf_op jit(solution)/shard_map/dot_general | solution.py:121
  (35 shorter events, 2.7 us)
Async XLA Ops:
  8.0 97.2 %all-reduce.3.cloned.1.call-start = ((), (), s32[]{:S(2)}) async-start(), calls=%async_computation.1 | async-start | bytes 10485760 | tf_op jit(solution)/shard_map/psum | solution.py:116
  15.6 2.5 %copy-start.1 = (bf16[512,128]{1,0:T(8,128)(2,1)S(1)}, bf16[512,128]{1,0:T(8,128)(2,1)}, u32[]{:S(2)}) copy-start(bf16[512,128]{1,0:T(8,128)(2,1)} %param.16) | copy-start | bytes 393220
  15.6 2.5 %copy-start.3 = (f32[128]{0:T(128)S(1)}, f32[128]{0:T(128)}, u32[]{:S(2)}) copy-start(f32[128]{0:T(128)} %param.19) | copy-start | bytes 1540
  18.1 2.1 %copy-start = (bf16[384,5120]{1,0:T(8,128)(2,1)S(1)}, bf16[384,5120]{1,0:T(8,128)(2,1)}, u32[]{:S(2)}) copy-start(bf16[384,5120]{1,0:T(8,128)(2,1)} %param.23) | copy-start | bytes 11796484
  25.0 24.8 %copy-start.2 = (s32[16,4]{0,1:T(4,128)S(1)}, s32[16,4]{0,1:T(4,128)}, u32[]{:S(2)}) copy-start(s32[16,4]{0,1:T(4,128)} %param.22) | copy-start | bytes 772
  25.0 89.9 %all-gather.3.cloned.1.call-start = ((), (), s32[]{:S(2)}) async-start(), calls=%async_computation.2 | async-start | bytes 9748480 | tf_op jit(solution)/shard_map/all_gather | solution.py:56
  25.6 165.4 %all-gather.5.cloned.1.call-start = ((), (), s32[]{:S(2)}) async-start(), calls=%async_computation.3 | async-start | bytes 9748480 | tf_op jit(solution)/shard_map/all_gather | solution.py:57
  41.2 27.5 %all-to-all-start = ((bf16[16,128,1,256]{3,1,2,0:T(8,128)(2,1)}), bf16[16,128,1,256]{3,1,2,0:T(8,128)(2,1)S(1)}, u32[]{:S(2)}, u32[]{:S(2)}) async-start(bf16[16,128,1,256]{3,1,2,0:T(8,128)(2,1)} %copy.89), calls=%async_computation | async-start | bytes 2097152 | tf_op jit(solution)/shard_map/all_to_all | solution.py:108
  70.1 44.8 %copy-start.4 = (f32[5120]{0:T(1024)S(1)}, f32[5120]{0:T(1024)}, u32[]{:S(2)}) copy-start(f32[5120]{0:T(1024)} %param.25) | copy-start | bytes 61444
Sparse Core Ops, SparseCore 0:
  25.1 80.0 all-reduce.2
Sparse Core Ops, SparseCore 1:
  27.6 87.3 all-gather.2
  116.9 74.0 all-gather.4
where the time goes:
time: 212 us; the launch traced here: 211 us
  waiting for transfers between devices  123 us (58%)
  matrix products  33.1 us (16%)
  between operations  23.5 us (11%)
  other arithmetic  16.9 us (8%)
  starting transfers between devices  8.73 us (4%)
  local copies, waits for them, and re-layouts  6.03 us (3%)
    all_gather x1, waiting for transfers between devices, shards(): wu_full = lax.all_gather(w_up, 'req', axis=0, tiled=True)  64 us
    psum x1, waiting for transfers between devices, shards(): lax.psum(jnp.dot(attended, w_out, preferred_element_type=jnp.float32).ast...  35 us
    all_to_all x1, waiting for transfers between devices, shards(): lax.all_to_all(kv_send, 'req', split_axis=0, concat_axis=0, tiled=True)  18.8 us
    dot_general x1, matrix products, shards(): up_acc = jnp.dot(normed, wu_full, preferred_element_type=jnp.float32)  12.7 us
    dot_general x1, matrix products, shards(): gate_acc = jnp.dot(normed, wg_full, preferred_element_type=jnp.float32)  12.1 us
    all_to_all x1, starting transfers between devices, shards(): lax.all_to_all(kv_send, 'req', split_axis=0, concat_axis=0, tiled=True)  8.61 us
    reduce_sum x1, other arithmetic, normalize(): scale_row = lax.rsqrt(jnp.mean(state * state, axis=-1, keepdims=True) + EPS)  5.83 us
    dot_general x1, matrix products, shards(): jnp.dot(attended, w_out, preferred_element_type=jnp.float32)  4.72 us
  transfers between devices with their start and end apart: 4, of which 4 were waited for; matrix products, arithmetic and copies ran while one was open for 13% of the time, Pallas kernels for 0%

commit v1 on v0

--- a/solution.py
+++ b/solution.py
@@ -54,7 +54,16 @@
     q_heads = q_pre.shape[1] // HD
     group_size = q_heads // kv_heads
     wg_full = lax.all_gather(w_gate, "req", axis=0, tiled=True)
-    wu_full = lax.all_gather(w_up, "req", axis=0, tiled=True)
+    ways = lax.axis_size("req")
+    up = [(d, (d + 1) % ways) for d in range(ways)]
+    down = [(d, (d - 1) % ways) for d in range(ways)]
+    earlier, later = ([w_up], [w_up])
+    for _ in range(ways // 2):
+        earlier.append(lax.ppermute(earlier[-1], "req", up))
+    for _ in range((ways - 1) // 2):
+        later.append(lax.ppermute(later[-1], "req", down))
+    line = jnp.concatenate([*earlier[::-1], *later[1:]], axis=0)
+    wu_full = jnp.roll(line, (lax.axis_index("req") - ways // 2) * w_up.shape[0], axis=0)
     own_lens = lax.dynamic_index_in_dim(lengths, me_req, 0, keepdims=False)
     own_pages = lax.dynamic_index_in_dim(page_table, me_req, 0, keepdims=False)
     own_owner = own_pages // REQS

time: 212 us -> 285 us (1.34); the launches traced: 211 us -> 281 us
  local copies, waits for them, and re-layouts: 6.03 us -> 53.1 us
  starting transfers between devices: 8.73 us -> 45.4 us
  waiting for transfers between devices: 123 us -> 107 us
    ppermute x0 -> x15, waiting for transfers between devices: none -> 107 us  [the longest x7 58.6 us: shards(): later.append(lax.ppermute(later[-1], 'req', down))]
    all_gather x1 -> x0, waiting for transfers between devices: 64 us -> none  [shards(): wu_full = lax.all_gather(w_up, 'req', axis=0, tiled=True)]
    unnamed x13 -> x50, local copies, waits for them, and re-layouts: 2.92 us -> 49.1 us
    ppermute x0 -> x15, starting transfers between devices: none -> 39.2 us  [the longest x7 37 us: shards(): later.append(lax.ppermute(later[-1], 'req', down))]
    psum x1, waiting for transfers between devices: 35 us -> 0.01 us  [shards(): lax.psum(jnp.dot(attended, w_out, preferred_element_type=jnp.float32).ast...]
    all_to_all x1, waiting for transfers between devices: 18.8 us -> 0.01 us  [shards(): lax.all_to_all(kv_send, 'req', split_axis=0, concat_axis=0, tiled=True)]
    all_gather x1, waiting for transfers between devices: 3.88 us -> 0.01 us  [shards(): wg_full = lax.all_gather(w_gate, 'req', axis=0, tiled=True)]
  transfers between devices with their start and end apart: 4 -> 18, of which waited for: 4 -> 11; matrix products, arithmetic and copies ran while one was open for 13% -> 22% of each run, Pallas kernels for 0% -> 0%
where the time goes in v1:
time: 285 us; the launch traced here: 281 us
  waiting for transfers between devices  107 us (38%)
  local copies, waits for them, and re-layouts  53.1 us (19%)
  starting transfers between devices  45.4 us (16%)
  matrix products  34.7 us (12%)
  between operations  23.4 us (8%)
  other arithmetic  17.1 us (6%)
    ppermute x7, waiting for transfers between devices, shards(): later.append(lax.ppermute(later[-1], 'req', down))  58.6 us
    unnamed x50, local copies, waits for them, and re-layouts  49.1 us
    ppermute x8, waiting for transfers between devices, shards(): earlier.append(lax.ppermute(earlier[-1], 'req', up))  48.1 us
    ppermute x7, starting transfers between devices, shards(): later.append(lax.ppermute(later[-1], 'req', down))  37 us
    dot_general x1, matrix products, shards(): up_acc = jnp.dot(normed, wu_full, preferred_element_type=jnp.float32)  13.4 us
    dot_general x1, matrix products, shards(): gate_acc = jnp.dot(normed, wg_full, preferred_element_type=jnp.float32)  12.1 us
    all_to_all x1, starting transfers between devices, shards(): lax.all_to_all(kv_send, 'req', split_axis=0, concat_axis=0, tiled=True)  6.16 us
    reduce_sum x1, other arithmetic, normalize(): scale_row = lax.rsqrt(jnp.mean(state * state, axis=-1, keepdims=True) + EPS)  5.83 us
  transfers between devices with their start and end apart: 18, of which 11 were waited for; matrix products, arithmetic and copies ran while one was open for 22% of the time, Pallas kernels for 0%

profile of v1, /device:TPU:1, one launch (start us, length us, event | category | flops | bytes accessed | tf_op | source)
XLA Modules:
  0.0 280.9 jit_solution(3184619685019200088)
XLA Ops:
  18.4 2.1 fusion.13
  20.5 4.7 %convolution_convert_fusion = bf16[512,5120]{1,0:T(8,128)(2,1)} fusion(bf16[512,384]{0,1:T(8,128)(2,1)S(1)} %bitcast.96, bf16[384,5120]{1,0:T(8,128)(2,1)S(1)} %copy-done), kind=kOutput, calls=%fused_computation.5 | convolution fusion | flops 2015887360 | bytes 9568256 | tf_op jit(solution)/shard_map/dot_general | solution.py:126
  25.8 2.2 collective-permute-start
  28.0 17.6 %collective-permute-done = bf16[320,864]{1,0:T(8,128)(2,1)S(1)} collective-permute-done((bf16[320,864]{1,0:T(8,128)(2,1)S(1)}, bf16[320,864]{1,0:T(8,128)(2,1)S(1)}, u32[]{:S(2)}, u32[]{:S(2)}) %collective-permute-start) | collective-permute-done | bytes 552992 | tf_op jit(solution)/shard_map/ppermute | solution.py:62
  45.6 4.8 %collective-permute-start.8 = (bf16[320,864]{1,0:T(8,128)(2,1)S(1)}, bf16[320,864]{1,0:T(8,128)(2,1)S(1)}, u32[]{:S(2)}, u32[]{:S(2)}) collective-permute-start(bf16[320,864]{1,0:T(8,128)(2,1)S(1)} %copy-done.1), channel_id=1, source_target_pairs={{0,120},{8,0},{16,8},{24,16},{32,24},{40,32},{48,40},{56,48},{64,5... | collective-permute-start | bytes 1658888 | tf_op jit(solution)/shard_map/ppermute | solution.py:64
  50.4 18.1 %collective-permute-done.1 = bf16[320,864]{1,0:T(8,128)(2,1)S(1)} collective-permute-done((bf16[320,864]{1,0:T(8,128)(2,1)S(1)}, bf16[320,864]{1,0:T(8,128)(2,1)S(1)}, u32[]{:S(2)}, u32[]{:S(2)}) %collective-permute-start.1) | collective-permute-done | bytes 552992 | tf_op jit(solution)/shard_map/ppermute | solution.py:62
  79.3 4.9 %collective-permute-start.9 = (bf16[320,864]{1,0:T(8,128)(2,1)S(1)}, bf16[320,864]{1,0:T(8,128)(2,1)}, u32[]{:S(2)}, u32[]{:S(2)}) collective-permute-start(bf16[320,864]{1,0:T(8,128)(2,1)S(1)} %collective-permute-done.8), channel_id=1, source_target_pairs={{0,120},{8,0},{16,8},{24,16},{32,24},{40,32},{48,40},{56,48},{64,5... | collective-permute-start | bytes 1658888 | tf_op jit(solution)/shard_map/ppermute | solution.py:64
  84.1 4.0 %collective-permute-done.2 = bf16[320,864]{1,0:T(8,128)(2,1)S(1)} collective-permute-done((bf16[320,864]{1,0:T(8,128)(2,1)S(1)}, bf16[320,864]{1,0:T(8,128)(2,1)S(1)}, u32[]{:S(2)}, u32[]{:S(2)}) %collective-permute-start.2) | collective-permute-done | bytes 552992 | tf_op jit(solution)/shard_map/ppermute | solution.py:62
  89.2 19.4 %collective-permute-done.9 = bf16[320,864]{1,0:T(8,128)(2,1)} collective-permute-done((bf16[320,864]{1,0:T(8,128)(2,1)S(1)}, bf16[320,864]{1,0:T(8,128)(2,1)}, u32[]{:S(2)}, u32[]{:S(2)}) %collective-permute-start.9) | collective-permute-done | bytes 552992 | tf_op jit(solution)/shard_map/ppermute | solution.py:64
  108.6 5.6 %collective-permute-start.10 = (bf16[320,864]{1,0:T(8,128)(2,1)}, bf16[320,864]{1,0:T(8,128)(2,1)}, u32[]{:S(2)}, u32[]{:S(2)}) collective-permute-start(bf16[320,864]{1,0:T(8,128)(2,1)} %collective-permute-done.9), channel_id=1, source_target_pairs={{0,120},{8,0},{16,8},{24,16},{32,24},{40,32},{48,40},{56,48},{64,5... | collective-permute-start | bytes 1658888 | tf_op jit(solution)/shard_map/ppermute | solution.py:64
  114.2 2.7 collective-permute-done.3
  119.8 6.2 %all-to-all-start = ((bf16[16,128,1,256]{3,1,2,0:T(8,128)(2,1)}), bf16[16,128,1,256]{3,1,2,0:T(8,128)(2,1)S(1)}, u32[]{:S(2)}, u32[]{:S(2)}) async-start(bf16[16,128,1,256]{3,1,2,0:T(8,128)(2,1)} %copy.89), calls=%async_computation | async-start | bytes 2097152 | tf_op jit(solution)/shard_map/all_to_all | solution.py:117
  126.0 11.3 %collective-permute-done.10 = bf16[320,864]{1,0:T(8,128)(2,1)} collective-permute-done((bf16[320,864]{1,0:T(8,128)(2,1)}, bf16[320,864]{1,0:T(8,128)(2,1)}, u32[]{:S(2)}, u32[]{:S(2)}) %collective-permute-start.10) | collective-permute-done | bytes 552992 | tf_op jit(solution)/shard_map/ppermute | solution.py:64
  137.4 5.8 %collective-permute-start.11 = (bf16[320,864]{1,0:T(8,128)(2,1)}, bf16[320,864]{1,0:T(8,128)(2,1)}, u32[]{:S(2)}, u32[]{:S(2)}) collective-permute-start(bf16[320,864]{1,0:T(8,128)(2,1)} %collective-permute-done.10), channel_id=1, source_target_pairs={{0,120},{8,0},{16,8},{24,16},{32,24},{40,32},{48,40},{56,48},{64,5... | collective-permute-start | bytes 1658888 | tf_op jit(solution)/shard_map/ppermute | solution.py:64
  143.1 4.5 %collective-permute-done.4 = bf16[320,864]{1,0:T(8,128)(2,1)} collective-permute-done((bf16[320,864]{1,0:T(8,128)(2,1)}, bf16[320,864]{1,0:T(8,128)(2,1)}, u32[]{:S(2)}, u32[]{:S(2)}) %collective-permute-start.4) | collective-permute-done | bytes 552992 | tf_op jit(solution)/shard_map/ppermute | solution.py:62
  147.6 14.9 %collective-permute-done.11 = bf16[320,864]{1,0:T(8,128)(2,1)} collective-permute-done((bf16[320,864]{1,0:T(8,128)(2,1)}, bf16[320,864]{1,0:T(8,128)(2,1)}, u32[]{:S(2)}, u32[]{:S(2)}) %collective-permute-start.11) | collective-permute-done | bytes 552992 | tf_op jit(solution)/shard_map/ppermute | solution.py:64
  162.5 5.0 %collective-permute-start.12 = (bf16[320,864]{1,0:T(8,128)(2,1)}, bf16[320,864]{1,0:T(8,128)(2,1)}, u32[]{:S(2)}, u32[]{:S(2)}) collective-permute-start(bf16[320,864]{1,0:T(8,128)(2,1)} %collective-permute-done.11), channel_id=1, source_target_pairs={{0,120},{8,0},{16,8},{24,16},{32,24},{40,32},{48,40},{56,48},{64,5... | collective-permute-start | bytes 1658888 | tf_op jit(solution)/shard_map/ppermute | solution.py:64
  170.2 8.5 %collective-permute-done.12 = bf16[320,864]{1,0:T(8,128)(2,1)} collective-permute-done((bf16[320,864]{1,0:T(8,128)(2,1)}, bf16[320,864]{1,0:T(8,128)(2,1)}, u32[]{:S(2)}, u32[]{:S(2)}) %collective-permute-start.12) | collective-permute-done | bytes 552992 | tf_op jit(solution)/shard_map/ppermute | solution.py:64
  178.7 5.5 %collective-permute-start.13 = (bf16[320,864]{1,0:T(8,128)(2,1)}, bf16[320,864]{1,0:T(8,128)(2,1)S(1)}, u32[]{:S(2)}, u32[]{:S(2)}) collective-permute-start(bf16[320,864]{1,0:T(8,128)(2,1)} %collective-permute-done.12), channel_id=1, source_target_pairs={{0,120},{8,0},{16,8},{24,16},{32,24},{40,32},{48,40},{56,48},{64,5... | collective-permute-start | bytes 1658888 | tf_op jit(solution)/shard_map/ppermute | solution.py:64
  184.2 5.8 %multiply_reduce_fusion = f32[512]{0:T(512)S(1)} fusion(bf16[512,5120]{1,0:T(8,128)(2,1)} %all-reduce.3.cloned.1.call-done, bf16[512,5120]{1,0:T(8,128)(2,1)} %param.24), kind=kLoop, calls=%fused_computation.1 | loop fusion | flops 13106688 | bytes 10487808 | tf_op jit(solution)/shard_map/reduce_sum | solution.py:30
  190.1 4.4 %collective-permute-done.13 = bf16[320,864]{1,0:T(8,128)(2,1)S(1)} collective-permute-done((bf16[320,864]{1,0:T(8,128)(2,1)}, bf16[320,864]{1,0:T(8,128)(2,1)S(1)}, u32[]{:S(2)}, u32[]{:S(2)}) %collective-permute-start.13) | collective-permute-done | bytes 552992 | tf_op jit(solution)/shard_map/ppermute | solution.py:64
  194.5 5.4 %collective-permute-start.14 = (bf16[320,864]{1,0:T(8,128)(2,1)S(1)}, bf16[320,864]{1,0:T(8,128)(2,1)S(1)}, u32[]{:S(2)}, u32[]{:S(2)}) collective-permute-start(bf16[320,864]{1,0:T(8,128)(2,1)S(1)} %collective-permute-done.13), channel_id=1, source_target_pairs={{0,120},{8,0},{16,8},{24,16},{32,24},{40,32},{48,40},{56,48},{64,5... | collective-permute-start | bytes 1658888 | tf_op jit(solution)/shard_map/ppermute | solution.py:64
  200.0 1.9 constant_dynamic-update-slice_fusion.31
  203.8 1.9 constant_dynamic-update-slice_fusion.29
  207.6 1.9 constant_dynamic-update-slice_fusion.27
  215.0 1.9 constant_dynamic-update-slice_fusion.21
  228.3 1.9 constant_dynamic-update-slice_fusion.13
  238.5 1.9 constant_dynamic-update-slice_fusion.5
  242.3 1.9 constant_dynamic-update-slice_fusion.3
  244.3 1.9 constant_dynamic-update-slice_fusion.2
  248.0 12.1 %fusion.63 = f32[512,864]{0,1:T(8,128)S(1)} fusion(bf16[5120,864]{1,0:T(8,128)(2,1)} %all-gather.2.cloned.1.call-done, bf16[512,5120]{1,0:T(8,128)(2,1)} %all-reduce.3.cloned.1.call-done, bf16[512,5120]{1,0:T(8,128)(2,1)} %param.24, f32[5120]{0:T(1024)S(1)} %copy-done.7, f32[512]{0:T(512)S(1)} %add_rsqrt_fusion), kind=kOutput, calls=%fused_computation.140 | convolution fusion | flops 4545576960 | bytes 21125120 | tf_op jit(solution)/shard_map/dot_general | solution.py:129
  260.0 13.4 %multiply_convert_fusion.1 = bf16[512,864]{0,1:T(8,128)(2,1)} fusion(f32[512,864]{0,1:T(8,128)S(1)} %fusion.63, bf16[10240,864]{1,0:T(8,128)(2,1)} %constant_dynamic-update-slice_fusion, s32[]{:T(128)S(6)} %select_n.108, bf16[512,5120]{1,0:T(8,128)(2,1)} %all-reduce.3.cloned.1.call-done, bf16[512,5120]{1,0:T(8,128)(2,1)} %param.24, f32[5120]{0:T(1024)S(1)} %copy-done.7, ...), kind=kOutput, calls=%fused_computation.13 | convolution fusion | flops 4548231168 | bytes 22337540 | tf_op jit(solution)/shard_map/dot_general | solution.py:130
  (100 shorter events, 53.2 us)
Async XLA Ops:
  8.0 176.2 %all-reduce.3.cloned.1.call-start = ((), (), s32[]{:S(2)}) async-start(), calls=%async_computation.1 | async-start | bytes 10485760 | tf_op jit(solution)/shard_map/psum | solution.py:125
  11.9 8.6 %copy-start = (bf16[384,5120]{1,0:T(8,128)(2,1)S(1)}, bf16[384,5120]{1,0:T(8,128)(2,1)}, u32[]{:S(2)}) copy-start(bf16[384,5120]{1,0:T(8,128)(2,1)} %param.23) | copy-start | bytes 11796484
  17.6 8.2 %copy-start.1 = (bf16[320,864]{1,0:T(8,128)(2,1)S(1)}, bf16[320,864]{1,0:T(8,128)(2,1)}, u32[]{:S(2)}) copy-start(bf16[320,864]{1,0:T(8,128)(2,1)} %param.27) | copy-start | bytes 1658884
  17.6 71.4 %copy-start.4 = (bf16[512,128]{1,0:T(8,128)(2,1)S(1)}, bf16[512,128]{1,0:T(8,128)(2,1)}, u32[]{:S(2)}) copy-start(bf16[512,128]{1,0:T(8,128)(2,1)} %param.16) | copy-start | bytes 393220
  17.6 71.4 %copy-start.6 = (f32[128]{0:T(128)S(1)}, f32[128]{0:T(128)}, u32[]{:S(2)}) copy-start(f32[128]{0:T(128)} %param.19) | copy-start | bytes 1540
  18.4 150.3 %copy-start.5 = (s32[16,4]{0,1:T(4,128)S(1)}, s32[16,4]{0,1:T(4,128)}, u32[]{:S(2)}) copy-start(s32[16,4]{0,1:T(4,128)} %param.22) | copy-start | bytes 772
  25.2 222.7 %all-gather.2.cloned.1.call-start = ((), (), s32[]{:S(2)}) async-start(), calls=%async_computation.2 | async-start | bytes 9748480 | tf_op jit(solution)/shard_map/all_gather | solution.py:56
  25.8 19.8 %collective-permute-start = (bf16[320,864]{1,0:T(8,128)(2,1)S(1)}, bf16[320,864]{1,0:T(8,128)(2,1)S(1)}, u32[]{:S(2)}, u32[]{:S(2)}) collective-permute-start(bf16[320,864]{1,0:T(8,128)(2,1)S(1)} %copy-done.1), channel_id=1, source_target_pairs={{0,8},{8,16},{16,24},{24,32},{32,40},{40,48},{48,56},{56,64},{64,7... | collective-permute-start | bytes 1658888 | tf_op jit(solution)/shard_map/ppermute | solution.py:62
  45.6 22.9 %collective-permute-start.1 = (bf16[320,864]{1,0:T(8,128)(2,1)S(1)}, bf16[320,864]{1,0:T(8,128)(2,1)S(1)}, u32[]{:S(2)}, u32[]{:S(2)}) collective-permute-start(bf16[320,864]{1,0:T(8,128)(2,1)S(1)} %collective-permute-done), channel_id=1, source_target_pairs={{0,8},{8,16},{16,24},{24,32},{32,40},{40,48},{48,56},{56,64},{64,7... | collective-permute-start | bytes 1658888 | tf_op jit(solution)/shard_map/ppermute | solution.py:62
  45.6 33.6 %collective-permute-start.8 = (bf16[320,864]{1,0:T(8,128)(2,1)S(1)}, bf16[320,864]{1,0:T(8,128)(2,1)S(1)}, u32[]{:S(2)}, u32[]{:S(2)}) collective-permute-start(bf16[320,864]{1,0:T(8,128)(2,1)S(1)} %copy-done.1), channel_id=1, source_target_pairs={{0,120},{8,0},{16,8},{24,16},{32,24},{40,32},{48,40},{56,48},{64,5... | collective-permute-start | bytes 1658888 | tf_op jit(solution)/shard_map/ppermute | solution.py:64
  68.5 19.7 %collective-permute-start.2 = (bf16[320,864]{1,0:T(8,128)(2,1)S(1)}, bf16[320,864]{1,0:T(8,128)(2,1)S(1)}, u32[]{:S(2)}, u32[]{:S(2)}) collective-permute-start(bf16[320,864]{1,0:T(8,128)(2,1)S(1)} %collective-permute-done.1), channel_id=1, source_target_pairs={{0,8},{8,16},{16,24},{24,32},{32,40},{40,48},{48,56},{56,64},{64,7... | collective-permute-start | bytes 1658888 | tf_op jit(solution)/shard_map/ppermute | solution.py:62
  79.3 29.3 %collective-permute-start.9 = (bf16[320,864]{1,0:T(8,128)(2,1)S(1)}, bf16[320,864]{1,0:T(8,128)(2,1)}, u32[]{:S(2)}, u32[]{:S(2)}) collective-permute-start(bf16[320,864]{1,0:T(8,128)(2,1)S(1)} %collective-permute-done.8), channel_id=1, source_target_pairs={{0,120},{8,0},{16,8},{24,16},{32,24},{40,32},{48,40},{56,48},{64,5... | collective-permute-start | bytes 1658888 | tf_op jit(solution)/shard_map/ppermute | solution.py:64
  88.2 31.7 %copy-start.2 = (bf16[320,864]{1,0:T(8,128)(2,1)}, bf16[320,864]{1,0:T(8,128)(2,1)S(1)}, u32[]{:S(2)}) copy-start(bf16[320,864]{1,0:T(8,128)(2,1)S(1)} %collective-permute-done.2) | copy-start | bytes 1658884
  88.2 28.7 %collective-permute-start.3 = (bf16[320,864]{1,0:T(8,128)(2,1)S(1)}, bf16[320,864]{1,0:T(8,128)(2,1)}, u32[]{:S(2)}, u32[]{:S(2)}) collective-permute-start(bf16[320,864]{1,0:T(8,128)(2,1)S(1)} %collective-permute-done.2), channel_id=1, source_target_pairs={{0,8},{8,16},{16,24},{24,32},{32,40},{40,48},{48,56},{56,64},{64,7... | collective-permute-start | bytes 1658888 | tf_op jit(solution)/shard_map/ppermute | solution.py:62
  108.6 28.8 %collective-permute-start.10 = (bf16[320,864]{1,0:T(8,128)(2,1)}, bf16[320,864]{1,0:T(8,128)(2,1)}, u32[]{:S(2)}, u32[]{:S(2)}) collective-permute-start(bf16[320,864]{1,0:T(8,128)(2,1)} %collective-permute-done.9), channel_id=1, source_target_pairs={{0,120},{8,0},{16,8},{24,16},{32,24},{40,32},{48,40},{56,48},{64,5... | collective-permute-start | bytes 1658888 | tf_op jit(solution)/shard_map/ppermute | solution.py:64
  116.9 30.7 %collective-permute-start.4 = (bf16[320,864]{1,0:T(8,128)(2,1)}, bf16[320,864]{1,0:T(8,128)(2,1)}, u32[]{:S(2)}, u32[]{:S(2)}) collective-permute-start(bf16[320,864]{1,0:T(8,128)(2,1)} %collective-permute-done.3), channel_id=1, source_target_pairs={{0,8},{8,16},{16,24},{24,32},{32,40},{40,48},{48,56},{56,64},{64,7... | collective-permute-start | bytes 1658888 | tf_op jit(solution)/shard_map/ppermute | solution.py:62
  119.8 48.9 %all-to-all-start = ((bf16[16,128,1,256]{3,1,2,0:T(8,128)(2,1)}), bf16[16,128,1,256]{3,1,2,0:T(8,128)(2,1)S(1)}, u32[]{:S(2)}, u32[]{:S(2)}) async-start(bf16[16,128,1,256]{3,1,2,0:T(8,128)(2,1)} %copy.89), calls=%async_computation | async-start | bytes 2097152 | tf_op jit(solution)/shard_map/all_to_all | solution.py:117
  137.4 25.2 %collective-permute-start.11 = (bf16[320,864]{1,0:T(8,128)(2,1)}, bf16[320,864]{1,0:T(8,128)(2,1)}, u32[]{:S(2)}, u32[]{:S(2)}) collective-permute-start(bf16[320,864]{1,0:T(8,128)(2,1)} %collective-permute-done.10), channel_id=1, source_target_pairs={{0,120},{8,0},{16,8},{24,16},{32,24},{40,32},{48,40},{56,48},{64,5... | collective-permute-start | bytes 1658888 | tf_op jit(solution)/shard_map/ppermute | solution.py:64
  147.6 21.1 %collective-permute-start.5 = (bf16[320,864]{1,0:T(8,128)(2,1)}, bf16[320,864]{1,0:T(8,128)(2,1)}, u32[]{:S(2)}, u32[]{:S(2)}) collective-permute-start(bf16[320,864]{1,0:T(8,128)(2,1)} %collective-permute-done.4), channel_id=1, source_target_pairs={{0,8},{8,16},{16,24},{24,32},{32,40},{40,48},{48,56},{56,64},{64,7... | collective-permute-start | bytes 1658888 | tf_op jit(solution)/shard_map/ppermute | solution.py:62
  162.5 16.2 %collective-permute-start.12 = (bf16[320,864]{1,0:T(8,128)(2,1)}, bf16[320,864]{1,0:T(8,128)(2,1)}, u32[]{:S(2)}, u32[]{:S(2)}) collective-permute-start(bf16[320,864]{1,0:T(8,128)(2,1)} %collective-permute-done.11), channel_id=1, source_target_pairs={{0,120},{8,0},{16,8},{24,16},{32,24},{40,32},{48,40},{56,48},{64,5... | collective-permute-start | bytes 1658888 | tf_op jit(solution)/shard_map/ppermute | solution.py:64
  168.7 15.6 %collective-permute-start.6 = (bf16[320,864]{1,0:T(8,128)(2,1)}, bf16[320,864]{1,0:T(8,128)(2,1)}, u32[]{:S(2)}, u32[]{:S(2)}) collective-permute-start(bf16[320,864]{1,0:T(8,128)(2,1)} %collective-permute-done.5), channel_id=1, source_target_pairs={{0,8},{8,16},{16,24},{24,32},{32,40},{40,48},{48,56},{56,64},{64,7... | collective-permute-start | bytes 1658888 | tf_op jit(solution)/shard_map/ppermute | solution.py:62
  169.5 64.6 %copy-start.3 = (bf16[320,864]{1,0:T(8,128)(2,1)S(1)}, bf16[320,864]{1,0:T(8,128)(2,1)}, u32[]{:S(2)}) copy-start(bf16[320,864]{1,0:T(8,128)(2,1)} %copy-done.2) | copy-start | bytes 1658884
  178.7 15.8 %collective-permute-start.13 = (bf16[320,864]{1,0:T(8,128)(2,1)}, bf16[320,864]{1,0:T(8,128)(2,1)S(1)}, u32[]{:S(2)}, u32[]{:S(2)}) collective-permute-start(bf16[320,864]{1,0:T(8,128)(2,1)} %collective-permute-done.12), channel_id=1, source_target_pairs={{0,120},{8,0},{16,8},{24,16},{32,24},{40,32},{48,40},{56,48},{64,5... | collective-permute-start | bytes 1658888 | tf_op jit(solution)/shard_map/ppermute | solution.py:64
  184.2 15.7 %collective-permute-start.7 = (bf16[320,864]{1,0:T(8,128)(2,1)}, bf16[320,864]{1,0:T(8,128)(2,1)}, u32[]{:S(2)}, u32[]{:S(2)}) collective-permute-start(bf16[320,864]{1,0:T(8,128)(2,1)} %collective-permute-done.6), channel_id=1, source_target_pairs={{0,8},{8,16},{16,24},{24,32},{32,40},{40,48},{48,56},{56,64},{64,7... | collective-permute-start | bytes 1658888 | tf_op jit(solution)/shard_map/ppermute | solution.py:62
  190.1 57.9 %copy-start.7 = (f32[5120]{0:T(1024)S(1)}, f32[5120]{0:T(1024)}, u32[]{:S(2)}) copy-start(f32[5120]{0:T(1024)} %param.25) | copy-start | bytes 61444
  194.5 29.0 %collective-permute-start.14 = (bf16[320,864]{1,0:T(8,128)(2,1)S(1)}, bf16[320,864]{1,0:T(8,128)(2,1)S(1)}, u32[]{:S(2)}, u32[]{:S(2)}) collective-permute-start(bf16[320,864]{1,0:T(8,128)(2,1)S(1)} %collective-permute-done.13), channel_id=1, source_target_pairs={{0,120},{8,0},{16,8},{24,16},{32,24},{40,32},{48,40},{56,48},{64,5... | collective-permute-start | bytes 1658888 | tf_op jit(solution)/shard_map/ppermute | solution.py:64
Sparse Core Ops, SparseCore 0:
  25.4 79.9 all-reduce.2
Sparse Core Ops, SparseCore 1:
  27.9 134.2 all-gather.1
